TPU v7x, 256 devices: a whole 4x4x8 slice. The times are simulated.
256 devices in a mesh: row: 8 (over y, x_lo), col: 32 (over x_hi, z, core).
Axes of the slice: x: 4 (x_hi: 2, x_lo: 2; x = x_hi * 2 + x_lo), y: 4, z: 8, core: 2. Of those that a mesh axis runs over, the one named last changes fastest.
Arguments:
- density: float32 [4096, 4096], P('row', 'col'), as said below
- pattern: int32 [32, 6], replicated, may hold values from 0 to 31, as said below
Outputs:
- purified: float32 [4096, 4096], P('row', 'col')
Inputs may be any that keep to these rules, and one draw needn't show every extreme that they name: density is symmetric. `pattern`: each row lists 6 different block columns; the first is the row's own index.
All inputs are finite; a program needn't handle non-finite values.
Results may differ from a plain program's by a relative error of at most 0.00021.
Values sent between devices are 32-bit elements; how exact they have to be, the bound alone decides.
No kernel may reach another device: no remote copies, remote signals or barrier semaphores. Data moves between devices by JAX's collectives and lax.ppermute only.
A program may use at most 64 MiB of HBM per device.

v0:
```python
import jax
import jax.numpy as jnp
from jax import lax
from jax.sharding import PartitionSpec as P

BLK = 128
NNZ = 6
ITERS = 2


def product(left, right):
    return jnp.dot(left, right, precision=lax.Precision.HIGH, preferred_element_type=jnp.float32)


def gather_rows(tile, name):
    parts = lax.axis_size(name)
    copies = jnp.broadcast_to(tile[None], (parts,) + tile.shape)
    got = lax.all_to_all(copies, name, 0, 0)
    return got.reshape(parts * tile.shape[0], tile.shape[1])


def local(density, pattern):
    rows_dev, cols_dev = density.shape
    row_number = lax.axis_index("row")
    col_index = lax.axis_index("col")
    matrix_order = cols_dev * lax.axis_size("col")
    block_count = matrix_order // BLK
    tile_blocks = cols_dev // BLK
    row_blocks = rows_dev // BLK
    listed = jnp.any(
        pattern[:, :, None] == jnp.arange(block_count, dtype=jnp.int32)[None, None, :], axis=1
    ).astype(jnp.float32)
    block_live = jnp.maximum(listed, listed.T)
    my_rows = lax.dynamic_slice_in_dim(block_live, row_number * row_blocks, row_blocks, 0)
    own_blocks = lax.dynamic_slice_in_dim(my_rows, col_index * tile_blocks, tile_blocks, 1)
    pattern_mask = jnp.repeat(jnp.repeat(own_blocks, BLK, axis=0), BLK, axis=1)
    global_rows = row_number * rows_dev + jnp.arange(rows_dev, dtype=jnp.int32)
    global_cols = col_index * cols_dev + jnp.arange(cols_dev, dtype=jnp.int32)
    identity = (global_rows[:, None] == global_cols[None, :]).astype(jnp.float32)
    current = 0.5 * identity + 0.45 / jnp.sqrt(jnp.float32(2 * NNZ * BLK)) * pattern_mask * density
    for purify_round in range(ITERS):
        row_panel = lax.all_gather(current, "col", axis=1, tiled=True)
        column_panel = gather_rows(current, "row")
        square = pattern_mask * product(row_panel, column_panel)
        square_panel = gather_rows(square, "row")
        cube = pattern_mask * product(row_panel, square_panel)
        current = 3.0 * square - 2.0 * cube
    return current


def solution(mesh):
    return jax.shard_map(
        local,
        mesh=mesh,
        in_specs=(P("row", "col"), P()),
        out_specs=P("row", "col"),
        check_vma=False,
    )
```

profile of v0, /device:TPU:1, one launch (start us, length us, event | category | flops | bytes accessed | tf_op | source)
XLA Modules:
  0.0 322.7 jit_solution(1169803695684405316)
XLA Ops:
  6.5 0.0 all-gather.3.cloned.1.call-start
  6.5 0.8 fusion.4
  7.4 0.1 dynamic_slice.8
  7.4 0.1 copy.6
  7.5 0.1 fusion.5
  7.6 0.1 bitcast_multiply_fusion
  7.7 1.9 multiply_add_fusion
  9.5 0.0 all-gather.3.cloned.1.call-update
  9.6 2.5 broadcast_in_dim.14
  12.0 5.9 %all-to-all-start = ((f32[8,512,128]{2,1,0:T(8,128)}), f32[8,512,128]{2,1,0:T(8,128)S(1)}, u32[]{:S(2)}, u32[]{:S(2)}) async-start(f32[8,512,128]{2,1,0:T(8,128)} %broadcast_in_dim.14), calls=%async_computation | async-start | bytes 4194304 | tf_op jit(solution)/shard_map/all_to_all | solution.py:18
  18.0 0.0 all-gather.5.cloned.1.call-start
  18.0 0.1 broadcast_bitcast_fusion
  18.1 28.8 %all-to-all-done = f32[8,512,128]{2,1,0:T(8,128)S(1)} async-done(((f32[8,512,128]{2,1,0:T(8,128)}), f32[8,512,128]{2,1,0:T(8,128)S(1)}, u32[]{:S(2)}, u32[]{:S(2)}) %all-to-all-start) | async-done | bytes 2097184 | tf_op jit(solution)/shard_map/all_to_all | solution.py:18
  46.8 78.6 %all-gather.3.cloned.1.call-done = f32[512,4096]{1,0:T(8,128)} async-done(((f32[512,128]{1,0:T(8,128)}), f32[512,4096]{1,0:T(8,128)}) %all-gather.3.cloned.1.call-update) | async-done | bytes 8388624 | tf_op jit(solution)/shard_map/all_gather | solution.py:42
  125.5 0.0 copy-start
  125.5 6.7 %convolution_multiply_fusion.3 = f32[512,128]{1,0:T(8,128)S(1)} fusion(f32[512,4096]{1,0:T(8,128)} %all-gather.3.cloned.1.call-done, f32[4096,128]{1,0:T(8,128)S(1)} %bitcast.19, f32[512]{0:T(512)S(1)} %broadcast_bitcast_fusion), kind=kOutput, calls=%fused_computation.5 | convolution fusion | flops 1610678272 | bytes 10749952 | tf_op jit(solution)/shard_map/dot_general | solution.py:12
  132.2 0.1 broadcast_in_dim.15
  132.3 30.0 %all_to_all.20 = f32[8,512,128]{2,1,0:T(8,128)S(1)} all-to-all(f32[8,512,128]{2,1,0:T(8,128)S(1)} %broadcast_in_dim.15), channel_id=1, replica_groups=mesh['row'=8,'col'=32] {'row'}, dimensions={0} | all-to-all | bytes 4194304 | tf_op jit(solution)/shard_map/all_to_all | solution.py:18
  162.4 0.0 copy-done
  162.4 4.2 %fusion.2 = f32[512,128]{1,0:T(8,128)} fusion(f32[512,4096]{1,0:T(8,128)S(1)} %copy-done, f32[4096,128]{1,0:T(8,128)S(1)} %bitcast.22, f32[512,128]{1,0:T(8,128)S(1)} %convolution_multiply_fusion.3, f32[512]{0:T(512)S(1)} %broadcast_bitcast_fusion), kind=kOutput, calls=%fused_computation.6 | convolution fusion | flops 1610874880 | bytes 11012096 | tf_op jit(solution)/shard_map/dot_general | solution.py:12
  166.5 0.0 all-gather.5.cloned.1.call-update
  166.6 1.1 broadcast_in_dim.16
  167.7 32.1 %all_to_all.21 = f32[8,512,128]{2,1,0:T(8,128)S(1)} all-to-all(f32[8,512,128]{2,1,0:T(8,128)S(1)} %broadcast_in_dim.16), channel_id=1, replica_groups=mesh['row'=8,'col'=32] {'row'}, dimensions={0} | all-to-all | bytes 4194304 | tf_op jit(solution)/shard_map/all_to_all | solution.py:18
  199.8 75.0 %all-gather.5.cloned.1.call-done = f32[512,4096]{1,0:T(8,128)} async-done(((f32[512,128]{1,0:T(8,128)}), f32[512,4096]{1,0:T(8,128)}) %all-gather.5.cloned.1.call-update) | async-done | bytes 8388624 | tf_op jit(solution)/shard_map/all_gather | solution.py:42
  274.8 0.0 copy-start.1
  274.8 6.7 %convolution_multiply_fusion.1 = f32[512,128]{1,0:T(8,128)S(1)} fusion(f32[512,4096]{1,0:T(8,128)} %all-gather.5.cloned.1.call-done, f32[4096,128]{1,0:T(8,128)S(1)} %bitcast.20, f32[512]{0:T(512)S(1)} %broadcast_bitcast_fusion), kind=kOutput, calls=%fused_computation.2 | convolution fusion | flops 1610678272 | bytes 10749952 | tf_op jit(solution)/shard_map/dot_general | solution.py:12
  281.5 0.1 broadcast_in_dim.17
  281.7 30.0 %all_to_all.22 = f32[8,512,128]{2,1,0:T(8,128)S(1)} all-to-all(f32[8,512,128]{2,1,0:T(8,128)S(1)} %broadcast_in_dim.17), channel_id=1, replica_groups=mesh['row'=8,'col'=32] {'row'}, dimensions={0} | all-to-all | bytes 4194304 | tf_op jit(solution)/shard_map/all_to_all | solution.py:18
  311.7 0.0 copy-done.1
  311.7 4.2 %fusion.3 = f32[512,128]{1,0:T(8,128)} fusion(f32[512,4096]{1,0:T(8,128)S(1)} %copy-done.1, f32[4096,128]{1,0:T(8,128)S(1)} %bitcast.21, f32[512,128]{1,0:T(8,128)S(1)} %convolution_multiply_fusion.1, f32[512]{0:T(512)S(1)} %broadcast_bitcast_fusion), kind=kOutput, calls=%fused_computation.7 | convolution fusion | flops 1610874880 | bytes 11012096 | tf_op jit(solution)/shard_map/dot_general | solution.py:12
  (3 shorter events, 0.0 us)
Async XLA Ops:
  6.5 118.9 %all-gather.3.cloned.1.call-start = ((), (), s32[]{:S(2)}) async-start(), calls=%async_computation.4 | async-start | bytes 8650752 | tf_op jit(solution)/shard_map/all_gather | solution.py:42
  12.0 34.8 %all-to-all-start = ((f32[8,512,128]{2,1,0:T(8,128)}), f32[8,512,128]{2,1,0:T(8,128)S(1)}, u32[]{:S(2)}, u32[]{:S(2)}) async-start(f32[8,512,128]{2,1,0:T(8,128)} %broadcast_in_dim.14), calls=%async_computation | async-start | bytes 4194304 | tf_op jit(solution)/shard_map/all_to_all | solution.py:18
  18.0 256.8 %all-gather.5.cloned.1.call-start = ((), (), s32[]{:S(2)}) async-start(), calls=%async_computation.5 | async-start | bytes 8650752 | tf_op jit(solution)/shard_map/all_gather | solution.py:42
  125.5 36.9 %copy-start = (f32[512,4096]{1,0:T(8,128)S(1)}, f32[512,4096]{1,0:T(8,128)}, u32[]{:S(2)}) copy-start(f32[512,4096]{1,0:T(8,128)} %all-gather.3.cloned.1.call-done) | copy-start | bytes 25165828
  274.8 36.9 %copy-start.1 = (f32[512,4096]{1,0:T(8,128)S(1)}, f32[512,4096]{1,0:T(8,128)}, u32[]{:S(2)}) copy-start(f32[512,4096]{1,0:T(8,128)} %all-gather.5.cloned.1.call-done) | copy-start | bytes 25165828
Sparse Core Ops, SparseCore 0:
  9.9 115.5 all-gather.2
  166.7 108.0 all-gather.4
where the time goes:
time: 323 us
  waiting for transfers between devices  182 us (56%)
  blocking collectives  92.2 us (29%)
  matrix products  21.7 us (7%)
  between operations  13.5 us (4%)
  starting transfers between devices  5.99 us (2%)
  local copies, waits for them, and re-layouts  4.07 us (1%)
    all_gather x2, waiting for transfers between devices, local(): row_panel = lax.all_gather(current, 'col', axis=1, tiled=True)  154 us
    all_to_all x3, blocking collectives, gather_rows(): got = lax.all_to_all(copies, name, 0, 0)  92.2 us
    all_to_all x1, waiting for transfers between devices, gather_rows(): got = lax.all_to_all(copies, name, 0, 0)  28.8 us
    dot_general x4, matrix products, product(): jnp.dot(left, right, precision=lax.Precision.HIGH, preferred_element_type...  21.7 us
  transfers between devices with their start and end apart: 3, of which 3 were waited for; matrix products, arithmetic and copies ran while one was open for 1% of the time, Pallas kernels for 0%

commit v1 on v0

--- a/solution.py
+++ b/solution.py
@@ -39,7 +39,9 @@
     identity = (global_rows[:, None] == global_cols[None, :]).astype(jnp.float32)
     current = 0.5 * identity + 0.45 / jnp.sqrt(jnp.float32(2 * NNZ * BLK)) * pattern_mask * density
     for purify_round in range(ITERS):
-        row_panel = lax.all_gather(current, "col", axis=1, tiled=True)
+        row_panel = jnp.concatenate(
+            lax.all_to_all(jnp.stack([current] * lax.axis_size("col")), "col", 0, 0), axis=1
+        )
         column_panel = gather_rows(current, "row")
         square = pattern_mask * product(row_panel, column_panel)
         square_panel = gather_rows(square, "row")

time: 323 us -> 559 us (1.73)
  blocking collectives: 92.2 us -> 255 us
  waiting for transfers between devices: 182 us -> 235 us
  starting transfers between devices: 5.99 us -> 22.3 us
  between operations: 13.5 us -> 0.12 us
  matrix products: 21.7 us -> 32.5 us
    all_to_all x0 -> x1, blocking collectives: none -> 200 us  [local(): lax.all_to_all(jnp.stack([current] * lax.axis_size('col')), 'col', 0, 0)]
    all_to_all x0 -> x1, waiting for transfers between devices: none -> 186 us  [local(): lax.all_to_all(jnp.stack([current] * lax.axis_size('col')), 'col', 0, 0)]
    all_gather x2 -> x0, waiting for transfers between devices: 154 us -> none  [local(): row_panel = lax.all_gather(current, 'col', axis=1, tiled=True)]
    all_to_all x3 -> x2, blocking collectives: 92.2 us -> 54.5 us  [gather_rows(): got = lax.all_to_all(copies, name, 0, 0)]
    all_to_all x1 -> x2, waiting for transfers between devices: 28.8 us -> 49.4 us  [gather_rows(): got = lax.all_to_all(copies, name, 0, 0)]
    all_to_all x0 -> x1, starting transfers between devices: none -> 12.7 us  [local(): lax.all_to_all(jnp.stack([current] * lax.axis_size('col')), 'col', 0, 0)]
    dot_general x4, matrix products: 21.7 us -> 32.5 us  [product(): jnp.dot(left, right, precision=lax.Precision.HIGH, preferred_element_type...]
  transfers between devices with their start and end apart: 3 -> 3, of which waited for: 3 -> 3; matrix products, arithmetic and copies ran while one was open for 1% -> 0% of each run, Pallas kernels for 0% -> 0%
where the time goes in v1:
time: 559 us; the launch traced here: 556 us
  blocking collectives  255 us (46%)
  waiting for transfers between devices  235 us (42%)
  matrix products  32.5 us (6%)
  starting transfers between devices  22.3 us (4%)
  local copies, waits for them, and re-layouts  9.05 us (2%)
    all_to_all x1, blocking collectives, local(): lax.all_to_all(jnp.stack([current] * lax.axis_size('col')), 'col', 0, 0)  200 us
    all_to_all x1, waiting for transfers between devices, local(): lax.all_to_all(jnp.stack([current] * lax.axis_size('col')), 'col', 0, 0)  186 us
    all_to_all x2, blocking collectives, gather_rows(): got = lax.all_to_all(copies, name, 0, 0)  54.5 us
    all_to_all x2, waiting for transfers between devices, gather_rows(): got = lax.all_to_all(copies, name, 0, 0)  49.4 us
    dot_general x4, matrix products, product(): jnp.dot(left, right, precision=lax.Precision.HIGH, preferred_element_type...  32.5 us
    all_to_all x1, starting transfers between devices, local(): lax.all_to_all(jnp.stack([current] * lax.axis_size('col')), 'col', 0, 0)  12.7 us
  transfers between devices with their start and end apart: 3, of which 3 were waited for; matrix products, arithmetic and copies ran while one was open for 0% of the time, Pallas kernels for 0%

profile of v1, /device:TPU:1, one launch (start us, length us, event | category | flops | bytes accessed | tf_op | source)
XLA Modules:
  0.0 555.5 jit_solution(10062860997380130297)
XLA Ops:
  0.0 0.8 fusion.4
  0.8 0.1 dynamic_slice.8
  0.9 0.1 copy.12
  1.0 0.1 fusion.5
  1.1 0.1 bitcast_multiply_fusion
  1.1 1.1 multiply_add_fusion
  2.3 1.5 broadcast_in_dim.14
  3.8 5.9 %all-to-all-start.1 = ((f32[8,512,128]{2,1,0:T(8,128)}), f32[8,512,128]{2,1,0:T(8,128)S(1)}, u32[]{:S(2)}, u32[]{:S(2)}) async-start(f32[8,512,128]{2,1,0:T(8,128)} %broadcast_in_dim.14), calls=%async_computation.1 | async-start | bytes 4194304 | tf_op jit(solution)/shard_map/all_to_all | solution.py:18
  9.7 0.1 copy.10
  9.8 25.9 %all-to-all-done.1 = f32[8,512,128]{2,1,0:T(8,128)S(1)} async-done(((f32[8,512,128]{2,1,0:T(8,128)}), f32[8,512,128]{2,1,0:T(8,128)S(1)}, u32[]{:S(2)}, u32[]{:S(2)}) %all-to-all-start.1) | async-done | bytes 2097184 | tf_op jit(solution)/shard_map/all_to_all | solution.py:18
  35.8 4.3 stack.4
  40.1 12.7 %all-to-all-start = ((f32[32,512,128]{1,2,0:T(8,128)}), f32[32,512,128]{1,2,0:T(8,128)}, u32[]{:S(2)}, u32[]{:S(2)}) async-start(f32[32,512,128]{1,2,0:T(8,128)} %stack.4), calls=%async_computation | async-start | bytes 16777216 | tf_op jit(solution)/shard_map/all_to_all | solution.py:43
  52.8 0.1 broadcast_bitcast_fusion
  52.9 185.5 %all-to-all-done = f32[32,512,128]{1,2,0:T(8,128)} async-done(((f32[32,512,128]{1,2,0:T(8,128)}), f32[32,512,128]{1,2,0:T(8,128)}, u32[]{:S(2)}, u32[]{:S(2)}) %all-to-all-start) | async-done | bytes 8388640 | tf_op jit(solution)/shard_map/all_to_all | solution.py:43
  238.4 9.1 %convolution_multiply_fusion.3 = f32[512,128]{1,0:T(8,128)S(1)} fusion(f32[512,4096]{0,1:T(8,128)} %bitcast.4, f32[4096,128]{1,0:T(8,128)S(1)} %bitcast.27, f32[512]{0:T(512)S(1)} %broadcast_bitcast_fusion), kind=kOutput, calls=%fused_computation.5 | convolution fusion | flops 1610678272 | bytes 10749952 | tf_op jit(solution)/shard_map/dot_general | solution.py:12
  247.4 0.1 broadcast_in_dim.15
  247.6 27.2 %all_to_all.30 = f32[8,512,128]{2,1,0:T(8,128)S(1)} all-to-all(f32[8,512,128]{2,1,0:T(8,128)S(1)} %broadcast_in_dim.15), channel_id=1, replica_groups=mesh['row'=8,'col'=32] {'row'}, dimensions={0} | all-to-all | bytes 4194304 | tf_op jit(solution)/shard_map/all_to_all | solution.py:18
  274.8 9.1 %fusion.2 = f32[512,128]{1,0:T(8,128)S(1)} fusion(f32[512,4096]{0,1:T(8,128)} %bitcast.4, f32[4096,128]{1,0:T(8,128)S(1)} %bitcast.30, f32[512,128]{1,0:T(8,128)S(1)} %convolution_multiply_fusion.3, f32[512]{0:T(512)S(1)} %broadcast_bitcast_fusion), kind=kOutput, calls=%fused_computation.6 | convolution fusion | flops 1610874880 | bytes 11012096 | tf_op jit(solution)/shard_map/dot_general | solution.py:12
  283.9 1.5 broadcast_in_dim.16
  285.4 3.6 all-to-all-start.4
  289.0 0.1 copy.11
  289.2 23.5 %all-to-all-done.4 = f32[8,512,128]{2,1,0:T(8,128)S(1)} async-done(((f32[8,512,128]{2,1,0:T(8,128)}), f32[8,512,128]{2,1,0:T(8,128)S(1)}, u32[]{:S(2)}, u32[]{:S(2)}) %all-to-all-start.4) | async-done | bytes 2097184 | tf_op jit(solution)/shard_map/all_to_all | solution.py:18
  312.6 1.1 stack.5
  313.7 200.0 %all_to_all.31 = f32[32,512,128]{1,2,0:T(8,128)S(1)} all-to-all(f32[32,512,128]{1,2,0:T(8,128)S(1)} %stack.5), channel_id=1, replica_groups=mesh['row'=8,'col'=32] {'col'}, dimensions={0} | all-to-all | bytes 16777216 | tf_op jit(solution)/shard_map/all_to_all | solution.py:43
  513.7 6.9 %convolution_multiply_fusion.1 = f32[512,128]{1,0:T(8,128)S(1)} fusion(f32[512,4096]{0,1:T(8,128)S(1)} %bitcast.25, f32[4096,128]{1,0:T(8,128)S(1)} %bitcast.28, f32[512]{0:T(512)S(1)} %broadcast_bitcast_fusion), kind=kOutput, calls=%fused_computation.2 | convolution fusion | flops 1610678272 | bytes 10749952 | tf_op jit(solution)/shard_map/dot_general | solution.py:12
  520.6 0.1 broadcast_in_dim.17
  520.7 27.3 %all_to_all.32 = f32[8,512,128]{2,1,0:T(8,128)S(1)} all-to-all(f32[8,512,128]{2,1,0:T(8,128)S(1)} %broadcast_in_dim.17), channel_id=1, replica_groups=mesh['row'=8,'col'=32] {'row'}, dimensions={0} | all-to-all | bytes 4194304 | tf_op jit(solution)/shard_map/all_to_all | solution.py:18
  548.1 7.5 %fusion.3 = f32[512,128]{1,0:T(8,128)} fusion(f32[512,4096]{0,1:T(8,128)S(1)} %bitcast.26, f32[4096,128]{1,0:T(8,128)S(1)} %bitcast.29, f32[512,128]{1,0:T(8,128)S(1)} %convolution_multiply_fusion.1, f32[512]{0:T(512)S(1)} %broadcast_bitcast_fusion), kind=kOutput, calls=%fused_computation.7 | convolution fusion | flops 1610874880 | bytes 11012096 | tf_op jit(solution)/shard_map/dot_general | solution.py:12
  (3 shorter events, 0.0 us)
Async XLA Ops:
  3.8 32.0 %all-to-all-start.1 = ((f32[8,512,128]{2,1,0:T(8,128)}), f32[8,512,128]{2,1,0:T(8,128)S(1)}, u32[]{:S(2)}, u32[]{:S(2)}) async-start(f32[8,512,128]{2,1,0:T(8,128)} %broadcast_in_dim.14), calls=%async_computation.1 | async-start | bytes 4194304 | tf_op jit(solution)/shard_map/all_to_all | solution.py:18
  40.1 198.3 %all-to-all-start = ((f32[32,512,128]{1,2,0:T(8,128)}), f32[32,512,128]{1,2,0:T(8,128)}, u32[]{:S(2)}, u32[]{:S(2)}) async-start(f32[32,512,128]{1,2,0:T(8,128)} %stack.4), calls=%async_computation | async-start | bytes 16777216 | tf_op jit(solution)/shard_map/all_to_all | solution.py:43
  285.4 27.2 %all-to-all-start.4 = ((f32[8,512,128]{2,1,0:T(8,128)}), f32[8,512,128]{2,1,0:T(8,128)S(1)}, u32[]{:S(2)}, u32[]{:S(2)}) async-start(f32[8,512,128]{2,1,0:T(8,128)} %broadcast_in_dim.16), calls=%async_computation.4 | async-start | bytes 4194304 | tf_op jit(solution)/shard_map/all_to_all | solution.py:18
